TPU v7x, 32 devices: a whole 2x2x4 slice. The times are simulated.
32 devices in a mesh: seq: 16 (over z, x, core), mlp: 2 (over y).
Axes of the slice: x: 2, y: 2, z: 4, core: 2. Of those that a mesh axis runs over, the one named last changes fastest.
Arguments:
- patches: bfloat16 [16384, 768], P(('seq', 'mlp')), may hold values from -6 to 6
- segments: int32 [16384], P(('seq', 'mlp')), may hold values from 0 to 5, as said below
- prompt_slots: int32 [16384], P(('seq', 'mlp')), may hold values from 0 to 50, as said below
- norm_gains: float32 [2, 2, 768], replicated, may hold values from 0.25 to 1.75
- qkv_weight: bfloat16 [2, 768, 2304], P(None, 'seq'), may hold values from -0.21875 to 0.21875
- out_weight: bfloat16 [2, 768, 768], P(None, 'seq'), may hold values from -0.875 to 0.875
- up_weight: bfloat16 [2, 768, 3072], P(None, 'seq', 'mlp'), may hold values from -0.21875 to 0.21875
- down_weight: bfloat16 [2, 3072, 768], P(None, 'mlp', 'seq'), may hold values from -0.15625 to 0.15625
- cotangent: bfloat16 [16384, 768], P(('seq', 'mlp')), may hold values from -6 to 6
- prompts: float32 [76800], P(('seq', 'mlp')), may hold values from -5 to 5
- first_moment: float32 [76800], P(('seq', 'mlp')), may hold values from -0.24 to 0.24
- second_moment: float32 [76800], P(('seq', 'mlp')), may hold values from 1e-05 to 0.015
- adam_betas: float32 [2], replicated, may hold values from 0.4 to 0.6
- learn_rate: float32 [1], replicated, may hold values from 0.2 to 0.6
Outputs:
- block_output: bfloat16 [16384, 768], P(('seq', 'mlp'))
- input_grad: float32 [16384, 768], P(('seq', 'mlp'))
- new_prompts: float32 [76800], P(('seq', 'mlp'))
- new_first: float32 [76800], P(('seq', 'mlp'))
- new_second: float32 [76800], P(('seq', 'mlp'))
- grad_norm: float32 [1], replicated
Inputs may be any that keep to these rules, and one draw needn't show every extreme that they name: `segments`: the 512 tokens of one device form aligned blocks in which whole images lie one after another, numbered 0, 1, 2 and so on; each image has 51 to 247 tokens, and every block holds an image of exactly 247 tokens. `prompt_slots`: the first 50 tokens of each image hold slots 0 to 49 in order; all other tokens hold 50.
All inputs are finite; a program needn't handle non-finite values.
Results may differ from a plain program's by a relative error of at most 0.02.
Values may be sent and summed in bfloat16 or wider, within the bound.
No kernel may reach another device: no remote copies, remote signals or barrier semaphores. Data moves between devices by JAX's collectives and lax.ppermute only.
A program may use at most 192 MiB of HBM per device.

v0:
```python
from functools import partial
import math
import jax
import jax.numpy as jnp
from jax import lax
from jax.sharding import PartitionSpec as P

HEADS = 12
HEAD_DIM = 64
ADAM_STEP = 2
ln_eps = 1e-06
masked_score = -1e30
clip_ratio = 0.05
adam_eps = 1e-08
decay_rate = 0.1
highest = lax.Precision.HIGHEST


def layer_norm(values, gain_row):
    center = values - jnp.mean(values, axis=-1, keepdims=True)
    spread = jnp.mean(center * center, axis=-1, keepdims=True)
    return center * lax.rsqrt(spread + ln_eps) * gain_row


def exact_gelu(values):
    return jax.nn.gelu(values, approximate=False)


def rows_times(piece_rows, weight):
    return jnp.dot(piece_rows, weight, preferred_element_type=jnp.float32)


def rows_times_back(piece_rows, weight):
    return jnp.einsum("td,fd->tf", piece_rows, weight, preferred_element_type=jnp.float32)


def slice_times(source, weight):
    return jnp.dot(source, weight, preferred_element_type=jnp.float32)


def slice_times_back(source, weight):
    return jnp.einsum("tf,df->td", source, weight, preferred_element_type=jnp.float32)


def masked_scores(query_rows, key_heads, seg_query, segments, score_scale):
    raw_scores = (
        jnp.einsum("qhd,khd->hqk", query_rows, key_heads, preferred_element_type=jnp.float32)
        * score_scale
    )
    allowed = (seg_query[:, None] == segments[None, :])[None]
    return jnp.where(allowed, raw_scores, masked_score)


def attend_forward(query_heads, key_heads, value_heads, segments, score_scale):
    tokens, head_count, head_depth = query_heads.shape
    block_rows = min(512, tokens)
    blocks = tokens // block_rows
    query_blocks = query_heads.reshape(blocks, block_rows, head_count, head_depth)
    seg_blocks = segments.reshape(blocks, block_rows)

    def one_block(block_pair):
        query_rows, seg_query = block_pair
        scores = masked_scores(query_rows, key_heads, seg_query, segments, score_scale)
        row_max = jnp.max(scores, axis=2, keepdims=True)
        exponent = jnp.exp(scores - row_max)
        row_total = jnp.sum(exponent, axis=2, keepdims=True)
        attn_probs = (exponent / row_total).astype(jnp.bfloat16)
        mixed_heads = jnp.einsum(
            "hqk,khd->qhd", attn_probs, value_heads, preferred_element_type=jnp.float32
        )
        return (mixed_heads.astype(jnp.bfloat16), row_max + jnp.log(row_total))

    mixed_heads, block_lse = lax.map(one_block, (query_blocks, seg_blocks))
    return (mixed_heads.reshape(tokens, head_count * head_depth), block_lse)


def attend_backward(
    query_heads, key_heads, value_heads, segments, block_lse, grad_mixed, score_scale
):
    tokens, head_count, head_depth = query_heads.shape
    block_rows = min(512, tokens)
    blocks = tokens // block_rows
    query_blocks = query_heads.reshape(blocks, block_rows, head_count, head_depth)
    grad_blocks = grad_mixed.reshape(blocks, block_rows, head_count, head_depth)
    seg_blocks = segments.reshape(blocks, block_rows)

    def one_block(running, block_parts):
        grad_keys, grad_values = running
        query_rows, grad_rows, seg_query, row_lse = block_parts
        scores = masked_scores(query_rows, key_heads, seg_query, segments, score_scale)
        attn_probs = jnp.exp(scores - row_lse)
        grad_probs = jnp.einsum(
            "qhd,khd->hqk", grad_rows, value_heads, preferred_element_type=jnp.float32
        )
        inner_sum = jnp.sum(attn_probs * grad_probs, axis=2, keepdims=True)
        grad_scores = (attn_probs * (grad_probs - inner_sum)).astype(jnp.bfloat16)
        grad_query = (
            jnp.einsum("hqk,khd->qhd", grad_scores, key_heads, preferred_element_type=jnp.float32)
            * score_scale
        )
        grad_keys = (
            grad_keys
            + jnp.einsum(
                "hqk,qhd->khd", grad_scores, query_rows, preferred_element_type=jnp.float32
            )
            * score_scale
        )
        grad_values = grad_values + jnp.einsum(
            "hqk,qhd->khd",
            attn_probs.astype(jnp.bfloat16),
            grad_rows,
            preferred_element_type=jnp.float32,
        )
        return ((grad_keys, grad_values), grad_query)

    zero_grads = jnp.zeros((tokens, head_count, head_depth), jnp.float32)
    (grad_keys, grad_values), grad_query = lax.scan(
        one_block, (zero_grads, zero_grads), (query_blocks, grad_blocks, seg_blocks, block_lse)
    )
    return (
        grad_query.reshape(tokens, head_count * head_depth),
        grad_keys.reshape(tokens, -1),
        grad_values.reshape(tokens, -1),
    )


def per_device(
    patches,
    segments,
    prompt_slots,
    norm_gains,
    qkv_weight,
    out_weight,
    up_weight,
    down_weight,
    cotangent,
    prompts,
    first_moment,
    second_moment,
    adam_betas,
    learn_rate,
):
    layers = norm_gains.shape[0]
    feature_width = norm_gains.shape[2]
    tokens = patches.shape[0]
    score_scale = HEAD_DIM ** (-0.5)
    gathered = lax.all_gather(prompts, ("seq", "mlp"), axis=0, tiled=True)
    prompt_table = gathered.reshape(layers, -1, feature_width)
    slot_total = prompt_table.shape[1]
    w_qkv, w_out, w_up, w_down = (
        lax.all_gather(qkv_weight, "seq", axis=1, tiled=True),
        lax.all_gather(out_weight, "seq", axis=1, tiled=True),
        lax.all_gather(up_weight, "seq", axis=1, tiled=True),
        lax.all_gather(down_weight, "seq", axis=2, tiled=True),
    )
    onehot = (prompt_slots[:, None] == jnp.arange(slot_total)[None, :]).astype(jnp.float32)
    is_prompt = (prompt_slots < slot_total)[:, None]
    hidden = patches.astype(jnp.float32)
    kept_state = []
    for layer_at in range(layers):
        inject = jnp.dot(onehot, prompt_table[layer_at], precision=highest)
        entry_rows = jnp.where(is_prompt, inject, hidden)
        normed_one, norm_one_back = jax.vjp(
            partial(layer_norm, gain_row=norm_gains[layer_at, 0]), entry_rows
        )
        qkv_proj = jnp.dot(
            normed_one.astype(jnp.bfloat16), w_qkv[layer_at], preferred_element_type=jnp.float32
        ).astype(jnp.bfloat16)
        query_heads = qkv_proj[:, :feature_width].reshape(tokens, HEADS, HEAD_DIM)
        key_heads = qkv_proj[:, feature_width : 2 * feature_width].reshape(tokens, HEADS, HEAD_DIM)
        value_heads = qkv_proj[:, 2 * feature_width :].reshape(tokens, HEADS, HEAD_DIM)
        mixed_rows, block_lse = attend_forward(
            query_heads, key_heads, value_heads, segments, score_scale
        )
        middle = entry_rows + jnp.dot(
            mixed_rows, w_out[layer_at], preferred_element_type=jnp.float32
        )
        normed_two, norm_two_back = jax.vjp(
            partial(layer_norm, gain_row=norm_gains[layer_at, 1]), middle
        )
        normed_low = normed_two.astype(jnp.bfloat16)
        before = rows_times(
            lax.all_gather(normed_low, "mlp", axis=0, tiled=True), weight=w_up[layer_at]
        )
        active = exact_gelu(before).astype(jnp.bfloat16)
        branch_two = lax.psum_scatter(
            slice_times(source=active, weight=w_down[layer_at]).astype(jnp.bfloat16),
            "mlp",
            scatter_dimension=0,
            tiled=True,
        ).astype(jnp.float32)
        hidden = middle + branch_two
        kept_state.append(
            (query_heads, key_heads, value_heads, block_lse, norm_one_back, norm_two_back, before)
        )
    block_output = hidden.astype(jnp.bfloat16)
    gradient = cotangent.astype(jnp.float32)
    layer_grads = []
    for layer_at in reversed(range(layers)):
        query_heads, key_heads, value_heads, block_lse, norm_one_back, norm_two_back, before = (
            kept_state[layer_at]
        )
        grad_low = gradient.astype(jnp.bfloat16)
        grad_active = rows_times_back(
            lax.all_gather(grad_low, "mlp", axis=0, tiled=True), weight=w_down[layer_at]
        )
        gelu_back = jax.vjp(exact_gelu, before)[1]
        grad_before = gelu_back(grad_active)[0].astype(jnp.bfloat16)
        grad_normtwo = lax.psum_scatter(
            slice_times_back(source=grad_before, weight=w_up[layer_at]).astype(jnp.bfloat16),
            "mlp",
            scatter_dimension=0,
            tiled=True,
        ).astype(jnp.float32)
        grad_middle = gradient + norm_two_back(grad_normtwo)[0]
        grad_branch = grad_middle.astype(jnp.bfloat16)
        grad_mixed = jnp.einsum(
            "te,de->td", grad_branch, w_out[layer_at], preferred_element_type=jnp.float32
        ).astype(jnp.bfloat16)
        grad_query, grad_keys, grad_values = attend_backward(
            query_heads,
            key_heads,
            value_heads,
            segments,
            block_lse,
            grad_mixed.reshape(tokens, HEADS, HEAD_DIM),
            score_scale,
        )
        grad_qkv = jnp.concatenate([grad_query, grad_keys, grad_values], axis=1).astype(
            jnp.bfloat16
        )
        grad_normone = jnp.einsum(
            "tc,dc->td", grad_qkv, w_qkv[layer_at], preferred_element_type=jnp.float32
        )
        grad_entry = grad_middle + norm_one_back(grad_normone)[0]
        layer_grads.append(jnp.einsum("tp,td->pd", onehot, grad_entry, precision=highest))
        gradient = jnp.where(is_prompt, 0.0, grad_entry)
    local_grads = jnp.stack(layer_grads[::-1]).reshape(-1)
    own_grads = lax.psum_scatter(local_grads, ("seq", "mlp"), scatter_dimension=0, tiled=True)
    square_sum = lax.psum(jnp.sum(own_grads * own_grads), ("seq", "mlp"))
    grad_norm = jnp.sqrt(square_sum)
    clip_limit = clip_ratio * math.sqrt(local_grads.shape[0])
    clipped = own_grads * jnp.minimum(1.0, clip_limit / (grad_norm + 1e-06))
    beta_one = adam_betas[0]
    beta_two = adam_betas[1]
    step_value = float(ADAM_STEP)
    new_first = beta_one * first_moment + (1.0 - beta_one) * clipped
    new_second = beta_two * second_moment + (1.0 - beta_two) * clipped * clipped
    first_hat = new_first / (1.0 - beta_one**step_value)
    second_hat = new_second / (1.0 - beta_two**step_value)
    new_prompts = prompts - learn_rate[0] * (
        first_hat / (jnp.sqrt(second_hat) + adam_eps) + decay_rate * prompts
    )
    return (block_output, gradient, new_prompts, new_first, new_second, grad_norm.reshape(1))


def solution(mesh):
    in_specs = (
        P(("seq", "mlp"), None),
        P(("seq", "mlp")),
        P(("seq", "mlp")),
        P(),
        P(None, "seq", None),
        P(None, "seq", None),
        P(None, "seq", "mlp"),
        P(None, "mlp", "seq"),
        P(("seq", "mlp"), None),
        P(("seq", "mlp")),
        P(("seq", "mlp")),
        P(("seq", "mlp")),
        P(),
        P(),
    )
    out_specs = (
        P(("seq", "mlp"), None),
        P(("seq", "mlp"), None),
        P(("seq", "mlp")),
        P(("seq", "mlp")),
        P(("seq", "mlp")),
        P(),
    )
    return jax.shard_map(
        per_device, mesh=mesh, in_specs=in_specs, out_specs=out_specs, check_vma=False
    )
```

profile of v0, /device:TPU:0, one launch (start us, length us, event | category | flops | bytes accessed | tf_op | source)
XLA Modules:
  0.0 815.6 jit_solution(11228677048224738187)
XLA Ops:
  14.0 175.3 %all-reduce.5.cloned.1.call-done = f32[76800]{0:T(1024)} async-done(((f32[76800]{0:T(1024)}), f32[76800]{0:T(1024)}) %all-reduce.5.cloned.1.call-update) | async-done | bytes 307216
  220.2 26.3 %all-gather.13.cloned.1.call-done = bf16[1024,768]{1,0:T(8,128)(2,1)} async-done(((bf16[512,768]{1,0:T(8,128)(2,1)}), bf16[1024,768]{1,0:T(8,128)(2,1)}) %all-gather.13.cloned.1.call-update) | async-done | bytes 1572880 | tf_op jit(solution)/shard_map/all_gather | solution.py:183
  246.6 19.2 %fusion.4 = (f32[1024,1536]{1,0:T(8,128)}, f32[1024,1536]{1,0:T(8,128)}) fusion(bf16[1024,768]{1,0:T(8,128)(2,1)} %all-gather.13.cloned.1.call-done, bf16[2,768,1536]{2,1,0:T(8,128)(2,1)} %all-gather.15.cloned.1.call-done), kind=kOutput, calls=%fused_computation.18 | convolution fusion | flops 2513436672 | bytes 16515072 | tf_op jit(solution)/shard_map/dot_general | solution.py:30
  265.8 36.5 %all-gather.17.cloned.1.call-done = bf16[2,1536,768]{1,2,0:T(8,128)(2,1)} async-done(((bf16[2,1536,48]{1,2,0:T(8,128)(2,1)}), bf16[2,1536,768]{1,2,0:T(8,128)(2,1)}) %all-gather.17.cloned.1.call-update) | async-done | bytes 4718608 | tf_op jit(solution)/shard_map/all_gather | solution.py:154
  302.3 9.1 %fusion.51 = bf16[1024,768]{1,0:T(8,128)(2,1)} fusion(bf16[2,1536,768]{1,2,0:T(8,128)(2,1)} %all-gather.17.cloned.1.call-done, f32[1024,1536]{1,0:T(8,128)} %get-tuple-element.152, f32[1024,1536]{1,0:T(8,128)} %get-tuple-element.153), kind=kOutput, calls=%fused_computation.95 | convolution fusion | flops 2421424128 | bytes 16515072 | tf_op jit(solution)/shard_map/dot_general | solution.py:38
  311.7 24.4 %reduce-scatter.5.cloned.1.call-done = bf16[512,768]{1,0:T(8,128)(2,1)} async-done(((bf16[1024,768]{1,0:T(8,128)(2,1)}), bf16[512,768]{1,0:T(8,128)(2,1)}) %reduce-scatter.5.cloned.1.call-update) | async-done | bytes 786448 | tf_op jit(solution)/shard_map/reduce_scatter | solution.py:186
  362.2 26.3 %all-gather.19.cloned.1.call-done = bf16[1024,768]{1,0:T(8,128)(2,1)} async-done(((bf16[512,768]{1,0:T(8,128)(2,1)}), bf16[1024,768]{1,0:T(8,128)(2,1)}) %all-gather.19.cloned.1.call-update) | async-done | bytes 1572880 | tf_op jit(solution)/shard_map/all_gather | solution.py:183
  388.6 18.9 %fusion.5 = (f32[1024,1536]{1,0:T(8,128)}, f32[1024,1536]{1,0:T(8,128)}) fusion(bf16[1024,768]{1,0:T(8,128)(2,1)} %all-gather.19.cloned.1.call-done, bf16[2,768,1536]{2,1,0:T(8,128)(2,1)} %all-gather.15.cloned.1.call-done), kind=kOutput, calls=%fused_computation.19 | convolution fusion | flops 2513436672 | bytes 16515072 | tf_op jit(solution)/shard_map/dot_general | solution.py:30
  407.4 9.7 %all-gather.21.cloned.1.call-done = bf16[1024,768]{1,0:T(8,128)(2,1)} async-done(((bf16[512,768]{1,0:T(8,128)(2,1)}), bf16[1024,768]{1,0:T(8,128)(2,1)}) %all-gather.21.cloned.1.call-update) | async-done | bytes 1572880 | tf_op jit(solution)/shard_map/all_gather | solution.py:205
  417.1 13.0 %fusion.49 = bf16[1024,768]{1,0:T(8,128)(2,1)} fusion(bf16[2,768,1536]{2,1,0:T(8,128)(2,1)} %all-gather.15.cloned.1.call-done, f32[1024,1536]{1,0:T(8,128)} %get-tuple-element.160, f32[1024,1536]{1,0:T(8,128)} %get-tuple-element.161, bf16[1024,768]{1,0:T(8,128)(2,1)} %all-gather.21.cloned.1.call-done, bf16[2,1536,768]{1,2,0:T(8,128)(2,1)} %all-gather.17.cloned.1.call-done), kind=kOutput, calls=%fused_computation.93 | convolution fusion | flops 4854644736 | bytes 20447232 | tf_op jit(solution)/shard_map/tf,df->td/dot_general | solution.py:42
  430.1 9.1 %fusion.50 = bf16[1024,768]{1,0:T(8,128)(2,1)} fusion(bf16[2,1536,768]{1,2,0:T(8,128)(2,1)} %all-gather.17.cloned.1.call-done, f32[1024,1536]{1,0:T(8,128)} %get-tuple-element.160, f32[1024,1536]{1,0:T(8,128)} %get-tuple-element.161), kind=kOutput, calls=%fused_computation.94 | convolution fusion | flops 2421424128 | bytes 16515072 | tf_op jit(solution)/shard_map/dot_general | solution.py:38
  439.7 16.4 %reduce-scatter.9.cloned.1.call-done = bf16[512,768]{1,0:T(8,128)(2,1)} async-done(((bf16[1024,768]{1,0:T(8,128)(2,1)}), bf16[512,768]{1,0:T(8,128)(2,1)}) %reduce-scatter.9.cloned.1.call-update) | async-done | bytes 786448 | tf_op jit(solution)/shard_map/reduce_scatter | solution.py:209
  457.7 26.8 %reduce-scatter.7.cloned.1.call-done = bf16[512,768]{1,0:T(8,128)(2,1)} async-done(((bf16[1024,768]{1,0:T(8,128)(2,1)}), bf16[512,768]{1,0:T(8,128)(2,1)}) %reduce-scatter.7.cloned.1.call-update) | async-done | bytes 786448 | tf_op jit(solution)/shard_map/reduce_scatter | solution.py:186
  491.3 7.3 fusion.52
  498.7 9.6 %multiply_reduce_fusion.1 = (f32[12,512]{1,0:T(8,128)S(1)}, f32[12,512,512]{1,2,0:T(8,128)}) fusion(f32[12,512]{1,0:T(8,128)S(1)} %log_add_fusion.1, f32[12,512,512]{1,2,0:T(8,128)} %copy-done.1, pred[512,512]{0,1:T(8,128)(4,1)S(1)} %broadcast_compare_fusion, bf16[512,12,64]{0,2,1:T(8,128)(2,1)S(1)} %bitcast.151, bf16[512,12,64]{0,2,1:T(8,128)(2,1)S(1)} %bitcast.149), kind=kOutput, calls=%fused_computation.4 | convolution fusion | flops 418375680 | bytes 27049984 | tf_op jit(solution)/shard_map/while/body/eval_jaxpr/qhd,khd->hqk/dot_general | solution.py:92
  508.3 7.1 multiply_convert_fusion.1
  524.6 26.9 %all-gather.23.cloned.1.call-done = bf16[1024,768]{1,0:T(8,128)(2,1)} async-done(((bf16[512,768]{1,0:T(8,128)(2,1)}), bf16[1024,768]{1,0:T(8,128)(2,1)}) %all-gather.23.cloned.1.call-update) | async-done | bytes 1572880 | tf_op jit(solution)/shard_map/all_gather | solution.py:205
  551.4 13.0 %fusion.48 = bf16[1024,768]{1,0:T(8,128)(2,1)} fusion(bf16[2,768,1536]{2,1,0:T(8,128)(2,1)} %all-gather.15.cloned.1.call-done, f32[1024,1536]{1,0:T(8,128)} %get-tuple-element.152, f32[1024,1536]{1,0:T(8,128)} %get-tuple-element.153, bf16[1024,768]{1,0:T(8,128)(2,1)} %all-gather.23.cloned.1.call-done, bf16[2,1536,768]{1,2,0:T(8,128)(2,1)} %all-gather.17.cloned.1.call-done), kind=kOutput, calls=%fused_computation.92 | convolution fusion | flops 4854644736 | bytes 20447232 | tf_op jit(solution)/shard_map/tf,df->td/dot_general | solution.py:42
  566.0 24.5 %reduce-scatter.11.cloned.1.call-done = bf16[512,768]{1,0:T(8,128)(2,1)} async-done(((bf16[1024,768]{1,0:T(8,128)(2,1)}), bf16[512,768]{1,0:T(8,128)(2,1)}) %reduce-scatter.11.cloned.1.call-update) | async-done | bytes 786448 | tf_op jit(solution)/shard_map/reduce_scatter | solution.py:209
  597.4 7.5 fusion.55
  604.9 9.5 %multiply_reduce_fusion = (f32[12,512]{1,0:T(8,128)S(1)}, f32[12,512,512]{1,2,0:T(8,128)}) fusion(f32[12,512]{1,0:T(8,128)S(1)} %log_add_fusion, f32[12,512,512]{1,2,0:T(8,128)} %copy-done, pred[512,512]{0,1:T(8,128)(4,1)S(1)} %broadcast_compare_fusion, bf16[512,12,64]{0,2,1:T(8,128)(2,1)S(1)} %bitcast.153, bf16[512,12,64]{0,2,1:T(8,128)(2,1)S(1)} %bitcast.147), kind=kOutput, calls=%fused_computation.1 | convolution fusion | flops 418375680 | bytes 27049984 | tf_op jit(solution)/shard_map/while/body/eval_jaxpr/qhd,khd->hqk/dot_general | solution.py:92
  614.5 7.1 multiply_convert_fusion
  637.0 120.7 %all-reduce.7.cloned.1.call-done = f32[76800]{0:T(1024)} async-done(((f32[76800]{0:T(1024)}), f32[76800]{0:T(1024)}) %all-reduce.7.cloned.1.call-update) | async-done | bytes 307216
  762.0 41.4 %psum.7 = f32[]{:T(128)} all-reduce(f32[]{:T(128)} %multiply_reduce_fusion.10), channel_id=1, replica_groups=mesh['seq'=16,'mlp'=2] {'seq','mlp'}, use_global_device_ids=true, to_apply=%region_28.29 | all-reduce | flops 1 | bytes 8 | tf_op jit(solution)/shard_map/psum | solution.py:240
  (245 shorter events, 106.8 us)
Async XLA Ops:
  8.0 181.4 %all-reduce.5.cloned.1.call-start = ((), (), s32[]{:S(2)}) async-start(), calls=%async_computation.16 | async-start | bytes 614400
  9.7 183.8 %all-gather.9.cloned.1.call-start = ((), (), s32[]{:S(2)}) async-start(), calls=%async_computation.4 | async-start | bytes 7520256 | tf_op jit(solution)/shard_map/all_gather | solution.py:151
  10.3 204.9 %all-gather.11.cloned.1.call-start = ((), (), s32[]{:S(2)}) async-start(), calls=%async_computation.5 | async-start | bytes 2506752 | tf_op jit(solution)/shard_map/all_gather | solution.py:152
  10.9 209.3 %all-gather.15.cloned.1.call-start = ((), (), s32[]{:S(2)}) async-start(), calls=%async_computation.7 | async-start | bytes 5013504 | tf_op jit(solution)/shard_map/all_gather | solution.py:153
  11.5 235.1 %all-gather.13.cloned.1.call-start = ((), (), s32[]{:S(2)}) async-start(), calls=%async_computation.6 | async-start | bytes 2359296 | tf_op jit(solution)/shard_map/all_gather | solution.py:183
  12.4 185.5 %copy-start.47 = (f32[768]{0:T(1024)}, f32[768]{0:T(1024)S(1)}, u32[]{:S(2)}) copy-start(f32[768]{0:T(1024)S(1)} %get-tuple-element.89) | copy-start | bytes 9220
  12.4 205.6 %copy-start.33 = (f32[768]{0:T(1024)}, f32[768]{0:T(1024)S(1)}, u32[]{:S(2)}) copy-start(f32[768]{0:T(1024)S(1)} %get-tuple-element.88) | copy-start | bytes 9220
  218.0 47.8 %copy-start.45 = (f32[512]{0:T(512)}, f32[512]{0:T(512)S(1)}, u32[]{:S(2)}) copy-start(f32[512]{0:T(512)S(1)} %multiply_reduce_fusion.8) | copy-start | bytes 6148
  219.4 82.9 %all-gather.17.cloned.1.call-start = ((), (), s32[]{:S(2)}) async-start(), calls=%async_computation.8 | async-start | bytes 5013504 | tf_op jit(solution)/shard_map/all_gather | solution.py:154
  220.2 115.9 %reduce-scatter.5.cloned.1.call-start = ((), (), s32[]{:S(2)}) async-start(), calls=%async_computation.9 | async-start | bytes 2359296 | tf_op jit(solution)/shard_map/reduce_scatter | solution.py:186
  311.4 77.2 %all-gather.19.cloned.1.call-start = ((), (), s32[]{:S(2)}) async-start(), calls=%async_computation.10 | async-start | bytes 2359296 | tf_op jit(solution)/shard_map/all_gather | solution.py:183
  361.4 55.7 %all-gather.21.cloned.1.call-start = ((), (), s32[]{:S(2)}) async-start(), calls=%async_computation.12 | async-start | bytes 2359296 | tf_op jit(solution)/shard_map/all_gather | solution.py:205
  362.0 94.2 %reduce-scatter.9.cloned.1.call-start = ((), (), s32[]{:S(2)}) async-start(), calls=%async_computation.13 | async-start | bytes 2359296 | tf_op jit(solution)/shard_map/reduce_scatter | solution.py:209
  430.1 54.4 %reduce-scatter.7.cloned.1.call-start = ((), (), s32[]{:S(2)}) async-start(), calls=%async_computation.11 | async-start | bytes 2359296 | tf_op jit(solution)/shard_map/reduce_scatter | solution.py:186
  439.3 112.2 %all-gather.23.cloned.1.call-start = ((), (), s32[]{:S(2)}) async-start(), calls=%async_computation.14 | async-start | bytes 2359296 | tf_op jit(solution)/shard_map/all_gather | solution.py:205
  524.3 66.2 %copy-start.34 = (f32[768]{0:T(1024)S(1)}, f32[768]{0:T(1024)}, u32[]{:S(2)}) copy-start(f32[768]{0:T(1024)} %copy-done.33) | copy-start | bytes 9220
  524.3 66.2 %copy-start.36 = (f32[512]{0:T(512)S(1)}, f32[512]{0:T(512)}, u32[]{:S(2)}) copy-start(f32[512]{0:T(512)} %copy-done.35) | copy-start | bytes 6148
  524.3 67.9 %copy-start.46 = (f32[512]{0:T(512)S(1)}, f32[512]{0:T(512)}, u32[]{:S(2)}) copy-start(f32[512]{0:T(512)} %copy-done.45) | copy-start | bytes 6148
  524.3 67.9 %copy-start.40 = (f32[512]{0:T(512)S(1)}, f32[512]{0:T(512)}, u32[]{:S(2)}) copy-start(f32[512]{0:T(512)} %copy-done.39) | copy-start | bytes 6148
  524.3 66.2 %reduce-scatter.11.cloned.1.call-start = ((), (), s32[]{:S(2)}) async-start(), calls=%async_computation.15 | async-start | bytes 2359296 | tf_op jit(solution)/shard_map/reduce_scatter | solution.py:209
  564.4 193.3 %all-reduce.7.cloned.1.call-start = ((), (), s32[]{:S(2)}) async-start(), calls=%async_computation.17 | async-start | bytes 614400
  628.4 175.7 %copy-start.38 = (f32[2400]{0:T(1024)S(1)}, f32[2400]{0:T(1024)}, u32[]{:S(2)}) copy-start(f32[2400]{0:T(1024)} %param.23) | copy-start | bytes 28804
  628.4 175.7 %copy-start.49 = (f32[2400]{0:T(1024)S(1)}, f32[2400]{0:T(1024)}, u32[]{:S(2)}) copy-start(f32[2400]{0:T(1024)} %param.25) | copy-start | bytes 28804
  628.4 175.7 %copy-start.50 = (f32[2400]{0:T(1024)S(1)}, f32[2400]{0:T(1024)}, u32[]{:S(2)}) copy-start(f32[2400]{0:T(1024)} %param.24) | copy-start | bytes 28804
  (56 other events, 476.8 us)
Sparse Core Ops, SparseCore 0:
  14.8 174.5 all-reduce.4
  632.1 125.6 all-reduce.6
Sparse Core Ops, SparseCore 1:
  12.5 69.7 all-gather.8
  84.4 41.0 all-gather.10
  127.6 52.1 all-gather.14
  219.5 27.0 all-gather.12
  249.1 53.1 all-gather.16
  311.5 24.5 reduce-scatter.4
  361.5 27.0 all-gather.18
  390.0 27.1 all-gather.20
  430.2 25.9 reduce-scatter.8
  458.5 25.9 reduce-scatter.6
  524.4 27.0 all-gather.22
  564.5 25.9 reduce-scatter.10
where the time goes:
time: 824 us; the launch traced here: 816 us
  waiting for transfers between devices  517 us (63%)
  matrix products  161 us (20%)
  other arithmetic  44.2 us (5%)
  blocking collectives  41.4 us (5%)
  local copies, waits for them, and re-layouts  27.1 us (3%)
  between operations  23.2 us (3%)
    unnamed x16, waiting for transfers between devices  299 us
    all_gather x2, waiting for transfers between devices, per_device(): lax.all_gather(normed_low, 'mlp', axis=0, tiled=True)  52.7 us
    reduce_scatter x2, waiting for transfers between devices, per_device(): lax.psum_scatter(slice_times(source=active, weight=w_down[layer_at]).asty...  51.2 us
    psum x1, blocking collectives, per_device(): square_sum = lax.psum(jnp.sum(own_grads * own_grads), ('seq', 'mlp'))  41.4 us
    reduce_scatter x2, waiting for transfers between devices, per_device(): lax.psum_scatter(slice_times_back(source=grad_before, weight=w_up[layer_a...  41 us
    dot_general x2, matrix products, rows_times(): return jnp.dot(piece_rows, weight, preferred_element_type=jnp.float32)  38.1 us
    all_gather x2, waiting for transfers between devices, per_device(): lax.all_gather(grad_low, 'mlp', axis=0, tiled=True)  36.5 us
    all_gather x1, waiting for transfers between devices, per_device(): lax.all_gather(down_weight, 'seq', axis=2, tiled=True)  36.5 us
  transfers between devices with their start and end apart: 14, of which 11 were waited for; matrix products, arithmetic and copies ran while one was open for 10% of the time, Pallas kernels for 0%

commit v1 on v0

--- a/solution.py
+++ b/solution.py
@@ -14,6 +14,30 @@
 adam_eps = 1e-08
 decay_rate = 0.1
 highest = lax.Precision.HIGHEST
+
+
+def slot_place(arr, ndim_at):
+    arr = jnp.moveaxis(arr, 0, ndim_at)
+    prior = arr.shape
+    return arr.reshape(*prior[:ndim_at], prior[ndim_at] * prior[ndim_at + 1], *prior[ndim_at + 2 :])
+
+
+def set_the_blocks(obj, chip_axis):
+    chips = lax.axis_size(chip_axis)
+    carry = obj[None]
+    for kk in range(chips.bit_length() - 1):
+        block_out = 1 << kk
+        field_out = lax.ppermute(
+            carry, chip_axis, list(map(lambda h: (h, h ^ block_out), range(chips)))
+        )
+        w1 = jnp.stack([carry, field_out], axis=0)
+        local_next = lax.axis_index(chip_axis) >> kk & 1
+        carry = jnp.where(local_next == 0, w1, w1[::-1]).reshape(-1, *obj.shape)
+    return carry
+
+
+def make_sites_on_mesh(packet, x_local, which_dim):
+    return slot_place(set_the_blocks(packet, x_local), which_dim)
 
 
 def layer_norm(values, gain_row):
@@ -180,7 +204,7 @@
         )
         normed_low = normed_two.astype(jnp.bfloat16)
         before = rows_times(
-            lax.all_gather(normed_low, "mlp", axis=0, tiled=True), weight=w_up[layer_at]
+            make_sites_on_mesh(normed_low, x_local="mlp", which_dim=0), weight=w_up[layer_at]
         )
         active = exact_gelu(before).astype(jnp.bfloat16)
         branch_two = lax.psum_scatter(

time: 824 us -> 773 us (0.938)
  waiting for transfers between devices: 517 us -> 465 us
    all_gather x2 -> x0, waiting for transfers between devices: 52.7 us -> none  [per_device(): lax.all_gather(normed_low, 'mlp', axis=0, tiled=True)]
    ppermute x0 -> x2, waiting for transfers between devices: none -> 43.9 us  [set_the_blocks(): lax.ppermute(carry, chip_axis, list(map(lambda h: (h, h ^ block_out), ran...]
    all_gather x1, waiting for transfers between devices: 36.5 us -> 0.01 us  [per_device(): lax.all_gather(down_weight, 'seq', axis=2, tiled=True)]
    all_gather x2, waiting for transfers between devices: 36.5 us -> 27.1 us  [per_device(): lax.all_gather(grad_low, 'mlp', axis=0, tiled=True)]
    unnamed x16 -> x14, waiting for transfers between devices: 299 us -> 299 us
  transfers between devices with their start and end apart: 14 -> 14, of which waited for: 11 -> 9; matrix products, arithmetic and copies ran while one was open for 10% -> 11% of each run, Pallas kernels for 0% -> 0%
where the time goes in v1:
time: 773 us; the launch traced here: 765 us
  waiting for transfers between devices  465 us (60%)
  matrix products  162 us (21%)
  other arithmetic  44.4 us (6%)
  blocking collectives  41.4 us (5%)
  local copies, waits for them, and re-layouts  25.7 us (3%)
  between operations  23.4 us (3%)
    unnamed x14, waiting for transfers between devices  299 us
    reduce_scatter x2, waiting for transfers between devices, per_device(): lax.psum_scatter(slice_times(source=active, weight=w_down[layer_at]).asty...  53.4 us
    ppermute x2, waiting for transfers between devices, set_the_blocks(): lax.ppermute(carry, chip_axis, list(map(lambda h: (h, h ^ block_out), ran...  43.9 us
    psum x1, blocking collectives, per_device(): square_sum = lax.psum(jnp.sum(own_grads * own_grads), ('seq', 'mlp'))  41.4 us
    reduce_scatter x2, waiting for transfers between devices, per_device(): lax.psum_scatter(slice_times_back(source=grad_before, weight=w_up[layer_a...  41.3 us
    dot_general x2, matrix products, rows_times(): return jnp.dot(piece_rows, weight, preferred_element_type=jnp.float32)  36.8 us
    all_gather x2, waiting for transfers between devices, per_device(): lax.all_gather(grad_low, 'mlp', axis=0, tiled=True)  27.1 us
    dot_general x2, matrix products, slice_times_back(): jnp.einsum('tf,df->td', source, weight, preferred_element_type=jnp.float32)  25.9 us
  transfers between devices with their start and end apart: 14, of which 9 were waited for; matrix products, arithmetic and copies ran while one was open for 11% of the time, Pallas kernels for 0%

profile of v1, /device:TPU:0, one launch (start us, length us, event | category | flops | bytes accessed | tf_op | source)
XLA Modules:
  0.0 764.6 jit_solution(17248771407965985237)
XLA Ops:
  14.8 175.8 %all-reduce.5.cloned.1.call-done = f32[76800]{0:T(1024)} async-done(((f32[76800]{0:T(1024)}), f32[76800]{0:T(1024)}) %all-reduce.5.cloned.1.call-update) | async-done | bytes 307216
  209.5 8.0 %fusion.59 = bf16[12,64,512]{2,1,0:T(8,128)(2,1)} fusion(bf16[512,12,64]{0,2,1:T(8,128)(2,1)S(1)} %bitcast.158, f32[12,512]{1,0:T(8,128)S(1)} %fusion, f32[12,512]{1,0:T(8,128)S(1)} %get-tuple-element.137, f32[12,512,512]{1,2,0:T(8,128)} %copy-done, pred[512,512]{0,1:T(8,128)(4,1)S(1)} %broadcast_compare_fusion), kind=kOutput, calls=%fused_computation.133 | convolution fusion | flops 418775040 | bytes 14467072 | tf_op jit(solution)/shard_map/while/body/eval_jaxpr/hqk,khd->qhd/dot_general | solution.py:92
  222.3 16.5 %collective-permute-done = bf16[1,512,768]{2,1,0:T(8,128)(2,1)S(1)} collective-permute-done((bf16[1,512,768]{2,1,0:T(8,128)(2,1)S(1)}, bf16[1,512,768]{2,1,0:T(8,128)(2,1)S(1)}, u32[]{:S(2)}, u32[]{:S(2)}) %collective-permute-start) | collective-permute-done | bytes 786464 | tf_op jit(solution)/shard_map/ppermute | solution.py:30
  239.4 18.4 %fusion.4 = (f32[1024,1536]{1,0:T(8,128)}, f32[1024,1536]{1,0:T(8,128)}) fusion(bf16[1024,768]{1,0:T(8,128)(2,1)S(1)} %bitcast.168, bf16[2,768,1536]{2,1,0:T(8,128)(2,1)} %all-gather.11.cloned.1.call-done), kind=kOutput, calls=%fused_computation.18 | convolution fusion | flops 2513436672 | bytes 16515072 | tf_op jit(solution)/shard_map/dot_general | solution.py:54
  257.8 9.1 %fusion.51 = bf16[1024,768]{1,0:T(8,128)(2,1)} fusion(bf16[2,1536,768]{1,2,0:T(8,128)(2,1)} %all-gather.13.cloned.1.call-done, f32[1024,1536]{1,0:T(8,128)} %get-tuple-element.152, f32[1024,1536]{1,0:T(8,128)} %get-tuple-element.153), kind=kOutput, calls=%fused_computation.97 | convolution fusion | flops 2421424128 | bytes 16515072 | tf_op jit(solution)/shard_map/dot_general | solution.py:62
  267.2 26.7 %reduce-scatter.5.cloned.1.call-done = bf16[512,768]{1,0:T(8,128)(2,1)} async-done(((bf16[1024,768]{1,0:T(8,128)(2,1)}), bf16[512,768]{1,0:T(8,128)(2,1)}) %reduce-scatter.5.cloned.1.call-update) | async-done | bytes 786448 | tf_op jit(solution)/shard_map/reduce_scatter | solution.py:210
  296.3 4.3 convolution_convert_fusion
  320.1 27.5 %collective-permute-done.1 = bf16[1,512,768]{2,1,0:T(8,128)(2,1)} collective-permute-done((bf16[1,512,768]{2,1,0:T(8,128)(2,1)}, bf16[1,512,768]{2,1,0:T(8,128)(2,1)}, u32[]{:S(2)}, u32[]{:S(2)}) %collective-permute-start.1) | collective-permute-done | bytes 786464 | tf_op jit(solution)/shard_map/ppermute | solution.py:30
  349.1 18.4 %fusion.5 = (f32[1024,1536]{1,0:T(8,128)}, f32[1024,1536]{1,0:T(8,128)}) fusion(bf16[1024,768]{1,0:T(8,128)(2,1)S(1)} %bitcast.169, bf16[2,768,1536]{2,1,0:T(8,128)(2,1)} %all-gather.11.cloned.1.call-done), kind=kOutput, calls=%fused_computation.19 | convolution fusion | flops 2513436672 | bytes 16515072 | tf_op jit(solution)/shard_map/dot_general | solution.py:54
  367.5 13.0 %fusion.49 = bf16[1024,768]{1,0:T(8,128)(2,1)} fusion(bf16[2,768,1536]{2,1,0:T(8,128)(2,1)} %all-gather.11.cloned.1.call-done, f32[1024,1536]{1,0:T(8,128)} %get-tuple-element.160, f32[1024,1536]{1,0:T(8,128)} %get-tuple-element.161, bf16[1024,768]{1,0:T(8,128)(2,1)} %all-gather.15.cloned.1.call-done, bf16[2,1536,768]{1,2,0:T(8,128)(2,1)} %all-gather.13.cloned.1.call-done), kind=kOutput, calls=%fused_computation.95 | convolution fusion | flops 4854644736 | bytes 20447232 | tf_op jit(solution)/shard_map/tf,df->td/dot_general | solution.py:66
  380.5 9.1 %fusion.50 = bf16[1024,768]{1,0:T(8,128)(2,1)} fusion(bf16[2,1536,768]{1,2,0:T(8,128)(2,1)} %all-gather.13.cloned.1.call-done, f32[1024,1536]{1,0:T(8,128)} %get-tuple-element.160, f32[1024,1536]{1,0:T(8,128)} %get-tuple-element.161), kind=kOutput, calls=%fused_computation.96 | convolution fusion | flops 2421424128 | bytes 16515072 | tf_op jit(solution)/shard_map/dot_general | solution.py:62
  390.1 16.6 %reduce-scatter.9.cloned.1.call-done = bf16[512,768]{1,0:T(8,128)(2,1)} async-done(((bf16[1024,768]{1,0:T(8,128)(2,1)}), bf16[512,768]{1,0:T(8,128)(2,1)}) %reduce-scatter.9.cloned.1.call-update) | async-done | bytes 786448 | tf_op jit(solution)/shard_map/reduce_scatter | solution.py:233
  408.3 26.8 %reduce-scatter.7.cloned.1.call-done = bf16[512,768]{1,0:T(8,128)(2,1)} async-done(((bf16[1024,768]{1,0:T(8,128)(2,1)}), bf16[512,768]{1,0:T(8,128)(2,1)}) %reduce-scatter.7.cloned.1.call-update) | async-done | bytes 786448 | tf_op jit(solution)/shard_map/reduce_scatter | solution.py:210
  440.5 7.3 fusion.52
  447.8 9.6 %multiply_reduce_fusion.1 = (f32[12,512]{1,0:T(8,128)S(1)}, f32[12,512,512]{1,2,0:T(8,128)}) fusion(f32[12,512]{1,0:T(8,128)S(1)} %log_add_fusion.1, f32[12,512,512]{1,2,0:T(8,128)} %copy-done.1, pred[512,512]{0,1:T(8,128)(4,1)S(1)} %broadcast_compare_fusion, bf16[512,12,64]{0,2,1:T(8,128)(2,1)S(1)} %bitcast.163, bf16[512,12,64]{0,2,1:T(8,128)(2,1)S(1)} %bitcast.161), kind=kOutput, calls=%fused_computation.4 | convolution fusion | flops 418375680 | bytes 27049984 | tf_op jit(solution)/shard_map/while/body/eval_jaxpr/qhd,khd->hqk/dot_general | solution.py:116
  457.4 7.1 multiply_convert_fusion.1
  474.6 27.1 %all-gather.17.cloned.1.call-done = bf16[1024,768]{1,0:T(8,128)(2,1)} async-done(((bf16[512,768]{1,0:T(8,128)(2,1)}), bf16[1024,768]{1,0:T(8,128)(2,1)}) %all-gather.17.cloned.1.call-update) | async-done | bytes 1572880 | tf_op jit(solution)/shard_map/all_gather | solution.py:229
  501.7 13.0 %fusion.48 = bf16[1024,768]{1,0:T(8,128)(2,1)} fusion(bf16[2,768,1536]{2,1,0:T(8,128)(2,1)} %all-gather.11.cloned.1.call-done, f32[1024,1536]{1,0:T(8,128)} %get-tuple-element.152, f32[1024,1536]{1,0:T(8,128)} %get-tuple-element.153, bf16[1024,768]{1,0:T(8,128)(2,1)} %all-gather.17.cloned.1.call-done, bf16[2,1536,768]{1,2,0:T(8,128)(2,1)} %all-gather.13.cloned.1.call-done), kind=kOutput, calls=%fused_computation.94 | convolution fusion | flops 4854644736 | bytes 20447232 | tf_op jit(solution)/shard_map/tf,df->td/dot_general | solution.py:66
  516.2 24.7 %reduce-scatter.11.cloned.1.call-done = bf16[512,768]{1,0:T(8,128)(2,1)} async-done(((bf16[1024,768]{1,0:T(8,128)(2,1)}), bf16[512,768]{1,0:T(8,128)(2,1)}) %reduce-scatter.11.cloned.1.call-update) | async-done | bytes 786448 | tf_op jit(solution)/shard_map/reduce_scatter | solution.py:233
  546.2 7.5 fusion.55
  553.8 9.5 %multiply_reduce_fusion = (f32[12,512]{1,0:T(8,128)S(1)}, f32[12,512,512]{1,2,0:T(8,128)}) fusion(f32[12,512]{1,0:T(8,128)S(1)} %log_add_fusion, f32[12,512,512]{1,2,0:T(8,128)} %copy-done, pred[512,512]{0,1:T(8,128)(4,1)S(1)} %broadcast_compare_fusion, bf16[512,12,64]{0,2,1:T(8,128)(2,1)S(1)} %bitcast.165, bf16[512,12,64]{0,2,1:T(8,128)(2,1)S(1)} %bitcast.159), kind=kOutput, calls=%fused_computation.1 | convolution fusion | flops 418375680 | bytes 27049984 | tf_op jit(solution)/shard_map/while/body/eval_jaxpr/qhd,khd->hqk/dot_general | solution.py:116
  563.3 7.1 multiply_convert_fusion
  585.9 120.7 %all-reduce.7.cloned.1.call-done = f32[76800]{0:T(1024)} async-done(((f32[76800]{0:T(1024)}), f32[76800]{0:T(1024)}) %all-reduce.7.cloned.1.call-update) | async-done | bytes 307216
  710.8 41.4 %psum.7 = f32[]{:T(128)} all-reduce(f32[]{:T(128)} %multiply_reduce_fusion.10), channel_id=1, replica_groups=mesh['seq'=16,'mlp'=2] {'seq','mlp'}, use_global_device_ids=true, to_apply=%region_28.29 | all-reduce | flops 1 | bytes 8 | tf_op jit(solution)/shard_map/psum | solution.py:264
  (259 shorter events, 96.2 us)
Async XLA Ops:
  8.0 182.6 %all-reduce.5.cloned.1.call-start = ((), (), s32[]{:S(2)}) async-start(), calls=%async_computation.14 | async-start | bytes 614400
  9.8 185.1 %all-gather.7.cloned.1.call-start = ((), (), s32[]{:S(2)}) async-start(), calls=%async_computation.4 | async-start | bytes 7520256 | tf_op jit(solution)/shard_map/all_gather | solution.py:175
  10.3 207.2 %all-gather.9.cloned.1.call-start = ((), (), s32[]{:S(2)}) async-start(), calls=%async_computation.5 | async-start | bytes 2506752 | tf_op jit(solution)/shard_map/all_gather | solution.py:176
  10.9 228.4 %all-gather.11.cloned.1.call-start = ((), (), s32[]{:S(2)}) async-start(), calls=%async_computation.6 | async-start | bytes 5013504 | tf_op jit(solution)/shard_map/all_gather | solution.py:177
  11.5 246.3 %all-gather.13.cloned.1.call-start = ((), (), s32[]{:S(2)}) async-start(), calls=%async_computation.7 | async-start | bytes 5013504 | tf_op jit(solution)/shard_map/all_gather | solution.py:178
  12.2 281.6 %reduce-scatter.5.cloned.1.call-start = ((), (), s32[]{:S(2)}) async-start(), calls=%async_computation.8 | async-start | bytes 2359296 | tf_op jit(solution)/shard_map/reduce_scatter | solution.py:210
  13.8 185.3 %copy-start.52 = (f32[768]{0:T(1024)}, f32[768]{0:T(1024)S(1)}, u32[]{:S(2)}) copy-start(f32[768]{0:T(1024)S(1)} %get-tuple-element.89) | copy-start | bytes 9220
  13.8 208.3 %copy-start.36 = (f32[768]{0:T(1024)}, f32[768]{0:T(1024)S(1)}, u32[]{:S(2)}) copy-start(f32[768]{0:T(1024)S(1)} %get-tuple-element.88) | copy-start | bytes 9220
  220.5 18.3 %collective-permute-start = (bf16[1,512,768]{2,1,0:T(8,128)(2,1)S(1)}, bf16[1,512,768]{2,1,0:T(8,128)(2,1)S(1)}, u32[]{:S(2)}, u32[]{:S(2)}) collective-permute-start(bf16[1,512,768]{2,1,0:T(8,128)(2,1)S(1)} %fusion.142), channel_id=1, source_target_pairs={{0,1},{1,0},{2,3},{3,2},{4,5},{5,4},{6,7},{7,6},{8,9},{9,8},{10,11... | collective-permute-start | bytes 2359304 | tf_op jit(solution)/shard_map/ppermute | solution.py:30
  266.9 100.6 %all-gather.15.cloned.1.call-start = ((), (), s32[]{:S(2)}) async-start(), calls=%async_computation.10 | async-start | bytes 2359296 | tf_op jit(solution)/shard_map/all_gather | solution.py:229
  319.2 28.3 %collective-permute-start.1 = (bf16[1,512,768]{2,1,0:T(8,128)(2,1)}, bf16[1,512,768]{2,1,0:T(8,128)(2,1)}, u32[]{:S(2)}, u32[]{:S(2)}) collective-permute-start(bf16[1,512,768]{2,1,0:T(8,128)(2,1)} %fusion.140), channel_id=1, source_target_pairs={{0,1},{1,0},{2,3},{3,2},{4,5},{5,4},{6,7},{7,6},{8,9},{9,8},{10,11... | collective-permute-start | bytes 2359304 | tf_op jit(solution)/shard_map/ppermute | solution.py:30
  319.5 87.2 %reduce-scatter.9.cloned.1.call-start = ((), (), s32[]{:S(2)}) async-start(), calls=%async_computation.11 | async-start | bytes 2359296 | tf_op jit(solution)/shard_map/reduce_scatter | solution.py:233
  380.5 54.6 %reduce-scatter.7.cloned.1.call-start = ((), (), s32[]{:S(2)}) async-start(), calls=%async_computation.9 | async-start | bytes 2359296 | tf_op jit(solution)/shard_map/reduce_scatter | solution.py:210
  389.6 112.0 %all-gather.17.cloned.1.call-start = ((), (), s32[]{:S(2)}) async-start(), calls=%async_computation.12 | async-start | bytes 2359296 | tf_op jit(solution)/shard_map/all_gather | solution.py:229
  474.3 40.5 %copy-start.8 = (f32[512,768]{1,0:T(8,128)}, f32[512,768]{1,0:T(8,128)S(1)}, u32[]{:S(2)}) copy-start(f32[512,768]{1,0:T(8,128)S(1)} %get-tuple-element.108) | copy-start | bytes 4718596
  474.3 40.4 %copy-start.35 = (f32[12,512]{1,0:T(8,128)S(1)}, f32[12,512]{1,0:T(8,128)}, u32[]{:S(2)}) copy-start(f32[12,512]{1,0:T(8,128)} %copy-done.34) | copy-start | bytes 73732
  474.3 40.4 %copy-start.39 = (f32[12,512]{1,0:T(8,128)S(1)}, f32[12,512]{1,0:T(8,128)}, u32[]{:S(2)}) copy-start(f32[12,512]{1,0:T(8,128)} %copy-done.38) | copy-start | bytes 73732
  474.3 66.6 %copy-start.37 = (f32[768]{0:T(1024)S(1)}, f32[768]{0:T(1024)}, u32[]{:S(2)}) copy-start(f32[768]{0:T(1024)} %copy-done.36) | copy-start | bytes 9220
  474.3 66.6 %copy-start.41 = (f32[512]{0:T(512)S(1)}, f32[512]{0:T(512)}, u32[]{:S(2)}) copy-start(f32[512]{0:T(512)} %copy-done.40) | copy-start | bytes 6148
  474.3 66.6 %reduce-scatter.11.cloned.1.call-start = ((), (), s32[]{:S(2)}) async-start(), calls=%async_computation.13 | async-start | bytes 2359296 | tf_op jit(solution)/shard_map/reduce_scatter | solution.py:233
  514.7 191.9 %all-reduce.7.cloned.1.call-start = ((), (), s32[]{:S(2)}) async-start(), calls=%async_computation.15 | async-start | bytes 614400
  579.0 173.9 %copy-start.45 = (f32[2400]{0:T(1024)S(1)}, f32[2400]{0:T(1024)}, u32[]{:S(2)}) copy-start(f32[2400]{0:T(1024)} %param.23) | copy-start | bytes 28804
  579.0 173.9 %copy-start.54 = (f32[2400]{0:T(1024)S(1)}, f32[2400]{0:T(1024)}, u32[]{:S(2)}) copy-start(f32[2400]{0:T(1024)} %param.25) | copy-start | bytes 28804
  579.0 173.9 %copy-start.55 = (f32[2400]{0:T(1024)S(1)}, f32[2400]{0:T(1024)}, u32[]{:S(2)}) copy-start(f32[2400]{0:T(1024)} %param.24) | copy-start | bytes 28804
  (61 other events, 442.6 us)
Sparse Core Ops, SparseCore 0:
  14.8 175.8 all-reduce.4
  267.0 26.7 reduce-scatter.4
  319.6 36.0 all-gather.14
  380.6 26.1 reduce-scatter.8
  408.9 26.0 reduce-scatter.6
  474.4 27.1 all-gather.16
  514.8 26.0 reduce-scatter.10
  580.9 125.6 all-reduce.6
Sparse Core Ops, SparseCore 1:
  12.8 69.7 all-gather.6
  84.9 41.2 all-gather.8
  128.6 52.4 all-gather.10
  183.7 51.6 all-gather.12
